TPU v7x, 512 devices: a whole 4x8x8 slice. The times are simulated.
512 devices in a mesh: slab: 16 (over z, core), col: 32 (over y, x).
Axes of the slice: x: 4, y: 8, z: 8, core: 2. Of those that a mesh axis runs over, the one named last changes fastest.
Arguments:
- field: bfloat16 [2, 256, 1024, 1024], P(None, 'slab', 'col'), may hold values from -6 to 6
- fine_plane: int32 [128, 1024, 1024], P('slab', 'col'), may hold values from 0 to 15, as said below
- fine_frac: int32 [128, 1024, 1024], P('slab', 'col'), may hold values from 0 to 7
- counts: int32 [16, 1024, 1024], P('slab', 'col'), may hold values from 1 to 8
Outputs:
- fine_color: float32 [1024, 1024], P('col', 'slab')
- fine_depth: float32 [1024, 1024], P('col', 'slab')
- coarse_color: float32 [1024, 1024], P('col', 'slab')
Inputs may be any that keep to these rules, and one draw needn't show every extreme that they name: For each ray and slab the positions 8 * fine_plane + fine_frac are nondecreasing over the 8 slots.
All inputs are finite; a program needn't handle non-finite values.
Results may differ from a plain program's by a relative error of at most 0.0003.
Values may be sent and summed in bfloat16 or wider, within the bound.
A program may use at most 64 MiB of HBM per device.

v0:
```python
import jax
import jax.numpy as jnp
from jax import lax
from jax.experimental import pallas as pl
from jax.experimental.pallas import tpu as pltpu
from jax.sharding import PartitionSpec as P

F32 = jnp.float32
MESH = pl.DeviceIdType.MESH
LANES = 128
HALF = 16
LOG2E = 1.4426950408889634
SHIFT = 0.5
TOP = 65535.0
COLOR_SPAN = (-22.5, 0.0)
DEPTH_SPAN = (-15.0, 10.75)


def pick(leaves, masks):
    for mask in masks:
        pairs = [jnp.where(mask, leaves[i + 1], leaves[i]) for i in range(0, len(leaves) - 1, 2)]
        leaves = pairs + leaves[2 * len(pairs) :]
    return leaves[0]


def softplus2(values):
    return jnp.log2(1.0 + jnp.exp2(values * LOG2E))


def march_group(field, halo, planes, fracs, counts, rows, cols, slab):
    depth = field.shape[1]
    slots = planes.shape[0]
    total = depth * 16
    scale = 2.0 / total

    def leaf(channel, plane):
        if plane == depth:
            return halo[channel, rows, cols]
        return field[channel, plane, rows, cols]

    shape = (HALF, LANES)
    live = counts[0, rows, cols]
    through, color, reach = jnp.ones(shape, F32), jnp.zeros(shape, F32), jnp.zeros(shape, F32)
    first = (slab * depth * 8).astype(F32) + SHIFT
    i16 = jnp.int16
    for slot in range(slots):
        plane = planes[slot, rows, cols]
        spot = (plane << 3) + fracs[slot, rows, cols]
        p = plane.astype(i16)
        up = p + i16(1)
        odd_bits = [(p & i16(2)) != i16(0), (p & i16(4)) != i16(0), p >= i16(8)]
        even_bits = [(up & i16(2)) != i16(0), (up & i16(4)) != i16(0), up >= i16(8), up >= i16(16)]
        even_weight = jnp.abs((spot & 15).astype(F32) * 0.125 - 1.0)
        values = []
        for channel in range(2):
            odd = pick([leaf(channel, k) for k in range(1, depth, 2)], odd_bits).astype(F32)
            even = pick([leaf(channel, k) for k in range(0, depth + 1, 2)], even_bits).astype(F32)
            values.append(odd + (even - odd) * even_weight)
        factor = jnp.exp2(softplus2(values[0]) * (-scale * depth / slots))
        after = through * jnp.where(live > slot, factor, 1.0)
        weight = through - after
        through = after
        color = color + weight * (1.0 + jnp.tanh(0.5 * values[1]))
        reach = reach + weight * (spot.astype(F32) + first)
    coarse_through, coarse = jnp.ones(shape, F32), jnp.zeros(shape, F32)
    for k in range(7, depth, 8):
        value, shine = [
            0.5 * (leaf(channel, k).astype(F32) + leaf(channel, k + 1).astype(F32)) for channel in range(2)
        ]
        after = coarse_through * jnp.exp2(softplus2(value) * (-8.0 * scale))
        coarse = coarse + (coarse_through - after) * (1.0 + jnp.tanh(0.5 * shine))
        coarse_through = after
    return 0.5 * color, reach, through, 0.5 * coarse, coarse_through


def as_code(u):
    return (jnp.clip(u, 0.0, TOP) + 0.5).astype(jnp.int32)


def encode_log(values, span):
    low, high = span
    step = TOP / (high - low)
    return as_code(jnp.log2(values) * step - low * step)


def decode_log(code, span):
    low, high = span
    return jnp.exp2(code.astype(F32) * ((high - low) / TOP) + low)


def kernel(
    field_in, plane_in, frac_in, count_in,
    image_out,
    field, halo, planes, fracs, counts, mine, sent, partner, packed, got, image,
    load_sem, halo_send, halo_recv, pair_send, pair_recv, chip_send, chip_recv, edge_send, edge_recv, behind, told,
):
    slab, col = lax.axis_index("slab"), lax.axis_index("col")
    slabs, columns = lax.axis_size("slab"), lax.axis_size("col")
    chips = slabs // 2
    z, core = slab // 2, slab % 2
    other = slab + 1 - 2 * core
    tiles = chips

    def device(s, c):
        return {"slab": s, "col": c}

    def order(chip, i):
        away = chips // 2 + jnp.where(i % 2 == 1, -1, 1) * ((i + 1) // 2)
        return lax.rem(chip + away, chips)

    def lanes(tile):
        return pl.ds(pl.multiple_of(tile * LANES, LANES), LANES)

    def loads(i):
        cols = lanes(order(z, i))
        return [
            pltpu.make_async_copy(field_in.at[:, :, :, cols], field.at[:, :, :, cols], load_sem.at[0, i]),
            pltpu.make_async_copy(plane_in.at[:, :, cols], planes.at[:, :, cols], load_sem.at[1, i]),
            pltpu.make_async_copy(frac_in.at[:, :, cols], fracs.at[:, :, cols], load_sem.at[2, i]),
            pltpu.make_async_copy(count_in.at[:, :, cols], counts.at[:, :, cols], load_sem.at[3, i]),
        ]

    barrier = pltpu.get_barrier_semaphore()

    def tell(semaphore, s, c):
        pl.semaphore_signal(semaphore, inc=1, device_id=device(s, c), device_id_type=MESH)

    tell(barrier, other, col)
    for away in range(1, chips):

        @pl.when(z < chips - away)
        def _():
            tell(barrier, slab + 2 * away, col)

    @pl.when(jnp.logical_and(core == 1, z < chips - 1))
    def _():
        tell(barrier, slab + 1, col)

    @pl.when(col > 0)
    def _():
        tell(barrier, 2 * z + 1, col - 1)

    @pl.when(col < columns - 1)
    def _():
        tell(barrier, 2 * z + 1, col + 1)

    for copy in loads(0):
        copy.start()

    def count(*conditions):
        return sum(jnp.where(c, 1, 0) for c in conditions)

    from_columns = 2 * core * count(col > 0, col < columns - 1)
    pl.semaphore_wait(barrier, 1 + z + (1 - core) * count(z > 0) + from_columns)

    def front_copy(to, i):
        cols = lanes(order(to // 2, i))
        return pltpu.make_async_remote_copy(
            src_ref=field_in.at[:, 0, :, cols], dst_ref=halo.at[:, :, cols],
            send_sem=halo_send.at[i], recv_sem=halo_recv.at[i],
            device_id=device(to, col), device_id_type=MESH,
        )

    @pl.when(slab > 0)
    def _():
        def start_front(i, _):
            front_copy(slab - 1, i).start()
            return 0

        lax.fori_loop(0, tiles, start_front, 0)

    for away in range(1, chips):

        @pl.when(z >= away)
        def _():
            tell(behind, slab - 2 * away, col)

    @pl.when(core == 1)
    def _():
        tell(told, other, col)

    def start_loads(i, _):
        for copy in loads(i):
            copy.start()
        return 0

    lax.fori_loop(1, tiles, start_loads, 0)

    @pl.when(slab == slabs - 1)
    def _():
        halo[...] = jnp.zeros_like(halo)

    patience = jnp.minimum(tiles, 3 * jnp.maximum(chips - 2 - z, 0))

    def hear_behind():
        pl.semaphore_wait(behind, chips - 1 - z)

    def pair_copy(i):
        return pltpu.make_async_remote_copy(
            src_ref=sent.at[i], dst_ref=partner.at[i],
            send_sem=pair_send.at[i], recv_sem=pair_recv.at[i],
            device_id=device(other, col), device_id_type=MESH,
        )

    def chip_copy(i):
        return pltpu.make_async_remote_copy(
            src_ref=packed.at[i], dst_ref=got.at[z],
            send_sem=chip_send.at[i], recv_sem=chip_recv.at[z],
            device_id=device(2 * order(z, i) + core, col), device_id_type=MESH,
        )

    def march(i, ref, half):
        rows = pl.ds(pl.multiple_of(half * HALF, HALF), HALF)
        parts = march_group(field, halo, planes, fracs, counts, rows, lanes(order(z, i)), slab)
        for n, part in enumerate(parts):
            ref[i, n] = part

    def join(i):
        pair_copy(i).wait_recv()
        words = []
        halves = []
        for rows in (pl.ds(0, 8), pl.ds(8, 8)):
            own = [mine[i, n, rows] for n in range(5)]
            far = [partner[i, n, rows] for n in range(5)]
            front = [jnp.where(core == 0, a, b) for a, b in zip(own, far)]
            back = [jnp.where(core == 0, b, a) for a, b in zip(own, far)]
            color = front[0] + front[2] * back[0]
            reach = front[1] + front[2] * back[1]
            coarse = front[3] + front[4] * back[3]
            halves.append([
                encode_log(color, COLOR_SPAN), encode_log(reach, DEPTH_SPAN), as_code(front[2] * back[2] * TOP),
                encode_log(coarse, COLOR_SPAN), as_code(front[4] * back[4] * TOP),
            ])
        for upper, lower in zip(*halves):
            words.append(upper | (lower << 16))
        return words

    def ready(i):
        for copy in loads(i):
            copy.wait()

        @pl.when(slab < slabs - 1)
        def _():
            front_copy(slab, i).wait_recv()

        march(i, sent, 1 - core)
        pair_copy(i).start()

    def step(i, _):
        ready(i + 1)
        march(i, mine, core)

        @pl.when(jnp.logical_and(i == patience, z < chips - 1))
        def _():
            hear_behind()

        for n, word in enumerate(join(i)):
            packed[i, n] = word

        @pl.when(jnp.logical_or(order(z, i) < z, i >= patience))
        def _():
            chip_copy(i).start()

        return 0

    ready(0)
    lax.fori_loop(0, tiles - 1, step, 0)
    march(tiles - 1, mine, core)

    @pl.when(patience >= tiles - 1)
    def _():
        hear_behind()

    def late(i, _):
        @pl.when(jnp.logical_and(order(z, i) > z, i < patience))
        def _():
            chip_copy(i).start()

        return 0

    lax.fori_loop(0, tiles - 1, late, 0)
    for n, word in enumerate(join(tiles - 1)):
        got[z, n] = word

    @pl.when(slab > 0)
    def _():
        def end_front(i, _):
            front_copy(slab - 1, i).wait_send()
            return 0

        lax.fori_loop(0, tiles, end_front, 0)

    def end_pair(i, _):
        pair_copy(i).wait_send()
        return 0

    lax.fori_loop(0, tiles, end_pair, 0)

    def end_chip(i, _):
        chip_copy(i).wait_send()
        return 0

    lax.fori_loop(0, tiles - 1, end_chip, 0)

    @pl.when(core == 0)
    def _():
        pl.semaphore_wait(told, 1)

    shape = (8, LANES)
    state = [[jnp.ones(shape, F32), jnp.ones(shape, F32)] + [jnp.zeros(shape, F32)] * 3 for _ in range(2)]
    for chip in range(chips):

        @pl.when(z != chip)
        def _():
            pltpu.make_async_remote_copy(
                src_ref=packed.at[0], dst_ref=got.at[chip], send_sem=chip_send.at[0], recv_sem=chip_recv.at[chip],
                device_id=device(slab, col), device_id_type=MESH,
            ).wait_recv()

        words = [got[chip, n] for n in range(5)]
        for half in range(2):
            codes = [(w & 0xFFFF) if half == 0 else (lax.shift_right_logical(w, 16)) for w in words]
            fine, plain, color, reach, coarse = state[half]
            color = color + fine * decode_log(codes[0], COLOR_SPAN)
            reach = reach + fine * decode_log(codes[1], DEPTH_SPAN)
            coarse = coarse + plain * decode_log(codes[3], COLOR_SPAN)
            fine = fine * (codes[2].astype(F32) * (1.0 / TOP))
            plain = plain * (codes[4].astype(F32) * (1.0 / TOP))
            state[half] = [fine, plain, color, reach, coarse]
    for half in range(2):
        fine, plain, color, reach, coarse = state[half]
        rows = pl.ds(pl.multiple_of(8 + core * HALF + 8 * half, 8), 8)
        image[0, rows] = color
        image[1, rows] = (reach - SHIFT * (1.0 - fine)) * (1.0 / 2048)
        image[2, rows] = coarse

    def rows_copy(n, first, target_first, count, s, c):
        return pltpu.make_async_remote_copy(
            src_ref=image.at[:, pl.ds(pl.multiple_of(first, 8), count)],
            dst_ref=image.at[:, pl.ds(pl.multiple_of(target_first, 8), count)],
            send_sem=edge_send.at[n], recv_sem=edge_recv.at[n if n == 0 else 1 + core],
            device_id=device(s, c), device_id_type=MESH,
        )

    across = rows_copy(0, 8 + core * HALF, 8 + core * HALF, HALF, other, col)
    target = col - 1 + 2 * core
    inside = jnp.logical_and(target >= 0, target < columns)
    borders = [rows_copy(1 + n, 8 + 24 * core, 40 - 40 * core, 8, 2 * z + n, target) for n in range(2)]

    @pl.when(inside)
    def _():
        for copy in borders:
            copy.start()

    across.start()

    blank = jnp.zeros((3, 8, LANES), F32)

    def border_wait(sender, first):
        pltpu.make_async_remote_copy(
            src_ref=image.at[:, pl.ds(first, 8)], dst_ref=image.at[:, pl.ds(first, 8)],
            send_sem=edge_send.at[0], recv_sem=edge_recv.at[1 + sender],
            device_id=device(slab, col), device_id_type=MESH,
        ).wait_recv()

    @pl.when(col == 0)
    def _():
        image[:, pl.ds(0, 8)] = blank

    @pl.when(col > 0)
    def _():
        border_wait(1, 0)

    @pl.when(col == columns - 1)
    def _():
        image[:, pl.ds(40, 8)] = blank

    @pl.when(col < columns - 1)
    def _():
        border_wait(0, 40)

    pltpu.make_async_remote_copy(
        src_ref=image.at[:, pl.ds(8, HALF)],
        dst_ref=image.at[:, pl.ds(pl.multiple_of(8 + (1 - core) * HALF, 8), HALF)],
        send_sem=edge_send.at[0], recv_sem=edge_recv.at[0],
        device_id=device(slab, col), device_id_type=MESH,
    ).wait_recv()

    image_out[...] = image[...]

    across.wait_send()

    @pl.when(inside)
    def _():
        for copy in borders:
            copy.wait_send()


def smooth_kernel(image, color_out, depth_out, coarse_out):
    core = lax.axis_index("slab") % 2
    for n, out in enumerate((color_out, depth_out, coarse_out)):
        smooth = 0.25 * image[n, pl.ds(7, 32)] + 0.5 * image[n, pl.ds(8, 32)] + 0.25 * image[n, pl.ds(9, 32)]
        turned = pltpu.roll(smooth, LANES // 2, 1)
        out[...] = jnp.where(core == 0, smooth, turned)[:, : LANES // 2]


def body(field, fine_plane, fine_frac, counts):
    channels, depth, rows, width = field.shape
    slots = fine_plane.shape[0]
    tiles = width // LANES
    dma = pltpu.SemaphoreType.DMA
    out = jax.ShapeDtypeStruct((rows, LANES // 2), F32)
    vmem = pl.BlockSpec(memory_space=pltpu.VMEM)
    anywhere = pl.BlockSpec(memory_space=pltpu.HBM)
    image = pl.pallas_call(
        kernel,
        out_shape=jax.ShapeDtypeStruct((3, rows + 16, LANES), F32),
        in_specs=[anywhere] * 4,
        out_specs=vmem,
        scratch_shapes=[
            pltpu.VMEM((channels, depth, rows, width), jnp.bfloat16),
            pltpu.VMEM((channels, rows, width), jnp.bfloat16),
            pltpu.VMEM((slots, rows, width), jnp.int32),
            pltpu.VMEM((slots, rows, width), jnp.int32),
            pltpu.VMEM((1, rows, width), jnp.int32),
            pltpu.VMEM((tiles, 5, HALF, LANES), F32),
            pltpu.VMEM((tiles, 5, HALF, LANES), F32),
            pltpu.VMEM((tiles, 5, HALF, LANES), F32),
            pltpu.VMEM((tiles, 5, 8, LANES), jnp.int32),
            pltpu.VMEM((tiles, 5, 8, LANES), jnp.int32),
            pltpu.VMEM((3, 48, LANES), F32),
            dma((4, tiles)),
            dma((tiles,)), dma((tiles,)),
            dma((tiles,)), dma((tiles,)),
            dma((tiles,)), dma((tiles,)),
            dma((3,)), dma((3,)),
            pltpu.SemaphoreType.REGULAR, pltpu.SemaphoreType.REGULAR,
        ],
        compiler_params=pltpu.CompilerParams(collective_id=0, has_side_effects=True, vmem_limit_bytes=56400000),
        name="render",
    )(field, fine_plane, fine_frac, counts)
    return pl.pallas_call(
        smooth_kernel,
        out_shape=(out, out, out),
        in_specs=[vmem],
        out_specs=(vmem, vmem, vmem),
        compiler_params=pltpu.CompilerParams(vmem_limit_bytes=4 << 20),
        name="smooth",
    )(image)


def solution(mesh):
    in_specs = (
        P(None, "slab", "col", None),
        P("slab", "col", None),
        P("slab", "col", None),
        P("slab", "col", None),
    )
    out_specs = (P("col", "slab"), P("col", "slab"), P("col", "slab"))
    return jax.shard_map(body, mesh=mesh, in_specs=in_specs, out_specs=out_specs, check_vma=False)
```

profile of v0, /device:TPU:31, one launch (start us, length us, event | category | flops | bytes accessed | tf_op | source)
XLA Modules:
  0.0 26.0 jit_solution(4078082628136264818)
XLA Ops:
  0.6 24.7 %render.1.image = f32[3,48,128]{2,1,0:T(8,128)S(1)} custom-call(bf16[2,16,32,1024]{3,2,1,0:T(8,128)(2,1)} %field_in.1, s32[8,32,1024]{2,1,0:T(8,128)} %plane_in.1, s32[8,32,1024]{2,1,0:T(8,128)} %frac_in.1, s32[1,32,1024]{2,1,0:T(8,128)} %count_in.1), custom_call_target="tpu_custom_call" | custom-call | tf_op jit(solution)/shard_map/render/pallas_call | solution.py:415
  25.3 0.7 %smooth.1 = (f32[32,64]{1,0:T(8,128)}, f32[32,64]{1,0:T(8,128)}, f32[32,64]{1,0:T(8,128)}) custom-call(f32[3,48,128]{2,1,0:T(8,128)S(1)} %render.1.image), custom_call_target="tpu_custom_call" | custom-call | tf_op jit(solution)/shard_map/smooth/pallas_call | solution.py:442
where the time goes:
time: 26.1 us; the launch traced here: 26 us
  Pallas kernels  25.4 us (97%)
  between operations  0.64 us (2%)
    pallas_call x1, Pallas kernels, body(): pl.pallas_call(kernel, out_shape=jax.ShapeDtypeStruct((3, rows + 16, LANE...  24.7 us
    pallas_call x1, Pallas kernels, body(): pl.pallas_call(smooth_kernel, out_shape=(out, out, out), in_specs=[vmem],...  0.69 us

commit v1 on v0

v1 whole, which is shorter than its diff:
```python
import jax
import jax.numpy as jnp
from jax import lax
from jax.experimental import pallas as pl
from jax.experimental.pallas import tpu as pltpu
from jax.sharding import PartitionSpec as P

F32 = jnp.float32
MESH = pl.DeviceIdType.MESH
LANES = 128
HALF = 16
LOG2E = 1.4426950408889634
SHIFT = 0.5
TOP = 65535.0
COLOR_SPAN = (-22.5, 0.0)
DEPTH_SPAN = (-15.0, 10.75)


def pick(leaves, masks):
    for mask in masks:
        pairs = [jnp.where(mask, leaves[i + 1], leaves[i]) for i in range(0, len(leaves) - 1, 2)]
        leaves = pairs + leaves[2 * len(pairs) :]
    return leaves[0]


def softplus2(values):
    return jnp.log2(1.0 + jnp.exp2(values * LOG2E))


def march_group(field, halo, planes, fracs, counts, rows, cols, slab):
    depth = field.shape[1]
    slots = planes.shape[0]
    total = depth * 16
    scale = 2.0 / total

    def leaf(channel, plane):
        if plane == depth:
            return halo[channel, rows, cols]
        return field[channel, plane, rows, cols]

    shape = (HALF, LANES)
    live = counts[0, rows, cols]
    through, color, reach = jnp.ones(shape, F32), jnp.zeros(shape, F32), jnp.zeros(shape, F32)
    first = (slab * depth * 8).astype(F32) + SHIFT
    i16 = jnp.int16
    for slot in range(slots):
        plane = planes[slot, rows, cols]
        spot = (plane << 3) + fracs[slot, rows, cols]
        p = plane.astype(i16)
        up = p + i16(1)
        odd_bits = [(p & i16(2)) != i16(0), (p & i16(4)) != i16(0), p >= i16(8)]
        even_bits = [(up & i16(2)) != i16(0), (up & i16(4)) != i16(0), up >= i16(8), up >= i16(16)]
        even_weight = jnp.abs((spot & 15).astype(F32) * 0.125 - 1.0)
        values = []
        for channel in range(2):
            odd = pick([leaf(channel, k) for k in range(1, depth, 2)], odd_bits).astype(F32)
            even = pick([leaf(channel, k) for k in range(0, depth + 1, 2)], even_bits).astype(F32)
            values.append(odd + (even - odd) * even_weight)
        factor = jnp.exp2(softplus2(values[0]) * (-scale * depth / slots))
        after = through * jnp.where(live > slot, factor, 1.0)
        weight = through - after
        through = after
        color = color + weight * (1.0 + jnp.tanh(0.5 * values[1]))
        reach = reach + weight * (spot.astype(F32) + first)
    coarse_through, coarse = jnp.ones(shape, F32), jnp.zeros(shape, F32)
    for k in range(7, depth, 8):
        value, shine = [
            0.5 * (leaf(channel, k).astype(F32) + leaf(channel, k + 1).astype(F32)) for channel in range(2)
        ]
        after = coarse_through * jnp.exp2(softplus2(value) * (-8.0 * scale))
        coarse = coarse + (coarse_through - after) * (1.0 + jnp.tanh(0.5 * shine))
        coarse_through = after
    return 0.5 * color, reach, through, 0.5 * coarse, coarse_through


def as_code(u):
    return (jnp.clip(u, 0.0, TOP) + 0.5).astype(jnp.int32)


def encode_log(values, span):
    low, high = span
    step = TOP / (high - low)
    return as_code(jnp.log2(values) * step - low * step)


def decode_log(code, span):
    low, high = span
    return jnp.exp2(code.astype(F32) * ((high - low) / TOP) + low)


def kernel(
    field_in, plane_in, frac_in, count_in,
    image_out,
    field, front, halo, planes, fracs, counts, pool, packed, got, border, border_got,
    load_sem, halo_send, halo_recv, pair_send, pair_recv, chip_send, chip_recv, border_send, border_recv, behind, told,
):
    slab, col = lax.axis_index("slab"), lax.axis_index("col")
    slabs, columns = lax.axis_size("slab"), lax.axis_size("col")
    chips = slabs // 2
    z, core = slab // 2, slab % 2
    other = slab + 1 - 2 * core
    tiles = chips

    def device(s, c):
        return {"slab": s, "col": c}

    def lanes(tile):
        return pl.ds(pl.multiple_of(tile * LANES, LANES), LANES)

    def loads(i):
        cols = lanes(i)
        return [
            pltpu.make_async_copy(field_in.at[:, :, :, cols], field.at[:, :, :, cols], load_sem.at[0, i]),
            pltpu.make_async_copy(plane_in.at[:, :, cols], planes.at[:, :, cols], load_sem.at[1, i]),
            pltpu.make_async_copy(frac_in.at[:, :, cols], fracs.at[:, :, cols], load_sem.at[2, i]),
            pltpu.make_async_copy(count_in.at[:, :, cols], counts.at[:, :, cols], load_sem.at[3, i]),
        ]

    barrier = pltpu.get_barrier_semaphore()

    def tell(semaphore, s, c):
        pl.semaphore_signal(semaphore, inc=1, device_id=device(s, c), device_id_type=MESH)

    first_plane = pltpu.make_async_copy(field_in.at[:, 0], front, load_sem.at[0, tiles])

    @pl.when(slab > 0)
    def _():
        first_plane.start()

    tell(barrier, other, col)

    @pl.when(jnp.logical_and(core == 1, z < chips - 1))
    def _():
        tell(barrier, slab + 1, col)

    for copy in loads(0):
        copy.start()

    def tell_behind(chip, _):
        tell(barrier, 2 * chip + core, col)
        return 0

    lax.fori_loop(z + 1, chips, tell_behind, 0)

    def both_sides(act):
        @pl.when(col > 0)
        def _():
            act(0, col - 1)

        @pl.when(col < columns - 1)
        def _():
            act(1, col + 1)

    def greet_side(side, c):
        def tell_beside(chip, _):
            tell(barrier, 2 * chip + 1, c)
            return 0

        lax.fori_loop(z, chips, tell_beside, 0)

    both_sides(greet_side)

    def count(*conditions):
        return sum(jnp.where(c, 1, 0) for c in conditions)

    sides = count(col > 0, col < columns - 1)
    pl.semaphore_wait(barrier, 1 + z + (1 - core) * count(z > 0) + core * 2 * (z + 1) * sides)

    def front_copy(to, i):
        cols = lanes(i)
        return pltpu.make_async_remote_copy(
            src_ref=front.at[:, :, cols], dst_ref=halo.at[:, :, cols],
            send_sem=halo_send.at[i], recv_sem=halo_recv.at[i],
            device_id=device(to, col), device_id_type=MESH,
        )

    @pl.when(slab > 0)
    def _():
        first_plane.wait()

        def start_front(i, _):
            front_copy(slab - 1, i).start()
            return 0

        lax.fori_loop(0, tiles, start_front, 0)

    def told_ahead(chip, _):
        tell(behind, 2 * chip + core, col)
        return 0

    def aside(side, c):
        def told_aside(chip, _):
            tell(behind, 2 * chip + core, c)
            return 0

        lax.fori_loop(0, z, told_aside, 0)

    lax.fori_loop(0, z, told_ahead, 0)

    @pl.when(core == 1)
    def _():
        tell(told, other, col)
        both_sides(aside)

    def start_loads(i, _):
        for copy in loads(i):
            copy.start()
        return 0

    lax.fori_loop(1, tiles, start_loads, 0)

    @pl.when(slab == slabs - 1)
    def _():
        halo[...] = jnp.zeros_like(halo)

    @pl.when(core == 0)
    def _():
        pl.semaphore_wait(told, 1)
        both_sides(aside)

    def pair_copy(i):
        return pltpu.make_async_remote_copy(
            src_ref=pool.at[i, 2], dst_ref=pool.at[i, core],
            send_sem=pair_send.at[i], recv_sem=pair_recv.at[i],
            device_id=device(other, col), device_id_type=MESH,
        )

    def chip_copy(i):
        return pltpu.make_async_remote_copy(
            src_ref=packed.at[i], dst_ref=got.at[z],
            send_sem=chip_send.at[i], recv_sem=chip_recv.at[z],
            device_id=device(2 * i + core, col), device_id_type=MESH,
        )

    def border_copy(i, side, c):
        return pltpu.make_async_remote_copy(
            src_ref=border.at[i], dst_ref=border_got.at[1 - side, z],
            send_sem=border_send.at[side, i], recv_sem=border_recv.at[1 - side, z],
            device_id=device(2 * i + core, c), device_id_type=MESH,
        )

    left = lax.broadcasted_iota(jnp.int32, (8, LANES), 1) < LANES // 2
    left_slot = jnp.where(core == 0, 0, 2)
    right_slot = jnp.where(core == 0, 2, 1)

    def march(i):
        for copy in loads(i):
            copy.wait()

        @pl.when(slab < slabs - 1)
        def _():
            front_copy(slab, i).wait_recv()

        parts = [
            march_group(field, halo, planes, fracs, counts, pl.ds(HALF * g, HALF), lanes(i), slab) for g in range(2)
        ]
        for n, (upper, lower) in enumerate(zip(*parts)):
            for m in range(2):
                up, down = upper[8 * m : 8 * m + 8], lower[8 * m : 8 * m + 8]
                pool[i, left_slot, n, pl.ds(8 * m, 8)] = jnp.where(left, up, pltpu.roll(down, LANES // 2, 1))
                pool[i, right_slot, n, pl.ds(8 * m, 8)] = jnp.where(left, pltpu.roll(up, LANES // 2, 1), down)
        pair_copy(i).start()

    def join(i):
        pair_copy(i).wait_recv()
        halves, edges = [], []
        for m in range(2):
            front = [pool[i, 0, n, pl.ds(8 * m, 8)] for n in range(5)]
            back = [pool[i, 1, n, pl.ds(8 * m, 8)] for n in range(5)]
            color = front[0] + front[2] * back[0]
            reach = front[1] + front[2] * back[1]
            coarse = front[3] + front[4] * back[3]
            fine, plain = front[2] * back[2], front[4] * back[4]
            halves.append([
                encode_log(color, COLOR_SPAN), encode_log(reach, DEPTH_SPAN), as_code(fine * TOP),
                encode_log(coarse, COLOR_SPAN), as_code(plain * TOP),
            ])
            edges.append([color, reach, fine, coarse, plain])
        for n, (first, last) in enumerate(zip(*edges)):
            border[i, pl.ds(n, 1)] = jnp.where(left[:1], first[:1], last[7:])
        words = [first | (last << 16) for first, last in zip(*halves)]

        @pl.when(i == z)
        def _():
            for n, word in enumerate(words):
                got[z, n] = word

        @pl.when(i != z)
        def _():
            for n, word in enumerate(words):
                packed[i, n] = word

    def send(i):
        @pl.when(i != z)
        def _():
            chip_copy(i).start()

        both_sides(lambda side, c: border_copy(i, side, c).start())

    def finish(i):
        join(i)

        @pl.when(i <= z)
        def _():
            send(i)

    def step(i, _):
        march(i)
        finish(i - 1)
        return 0

    march(0)
    lax.fori_loop(1, tiles, step, 0)
    finish(tiles - 1)

    @pl.when(z < chips - 1)
    def _():
        pl.semaphore_wait(behind, (chips - 1 - z) * (1 + sides))

        def send_behind(i, _):
            send(i)
            return 0

        lax.fori_loop(z + 1, chips, send_behind, 0)

    @pl.when(slab > 0)
    def _():
        def end_front(i, _):
            front_copy(slab - 1, i).wait_send()
            return 0

        lax.fori_loop(0, tiles, end_front, 0)

    def end_tile(i, _):
        pair_copy(i).wait_send()

        @pl.when(i != z)
        def _():
            chip_copy(i).wait_send()

        both_sides(lambda side, c: border_copy(i, side, c).wait_send())
        return 0

    lax.fori_loop(0, tiles, end_tile, 0)

    shape = (8, LANES)
    state = [[jnp.ones(shape, F32), jnp.ones(shape, F32)] + [jnp.zeros(shape, F32)] * 3 for _ in range(2)]
    for chip in range(chips):

        @pl.when(z != chip)
        def _():
            pltpu.make_async_remote_copy(
                src_ref=packed.at[0], dst_ref=got.at[chip], send_sem=chip_send.at[0], recv_sem=chip_recv.at[chip],
                device_id=device(slab, col), device_id_type=MESH,
            ).wait_recv()

        words = [got[chip, n] for n in range(5)]
        for half in range(2):
            codes = [(w & 0xFFFF) if half == 0 else (lax.shift_right_logical(w, 16)) for w in words]
            fine, plain, color, reach, coarse = state[half]
            color = color + fine * decode_log(codes[0], COLOR_SPAN)
            reach = reach + fine * decode_log(codes[1], DEPTH_SPAN)
            coarse = coarse + plain * decode_log(codes[3], COLOR_SPAN)
            fine = fine * (codes[2].astype(F32) * (1.0 / TOP))
            plain = plain * (codes[4].astype(F32) * (1.0 / TOP))
            state[half] = [fine, plain, color, reach, coarse]
    for half in range(2):
        fine, plain, color, reach, coarse = state[half]
        rows = pl.ds(8 * half, 8)
        image_out[0, rows] = color
        image_out[1, rows] = (reach - SHIFT * (1.0 - fine)) * (1.0 / 2048)
        image_out[2, rows] = coarse

    def border_waits(side, c):
        for chip in range(chips):
            pltpu.make_async_remote_copy(
                src_ref=border.at[0], dst_ref=border_got.at[side, chip],
                send_sem=border_send.at[side, 0], recv_sem=border_recv.at[side, chip],
                device_id=device(slab, c), device_id_type=MESH,
            ).wait_recv()

    both_sides(border_waits)
    line = (1, LANES)
    fine, plain = jnp.ones(line, F32), jnp.ones(line, F32)
    color, reach, coarse = [jnp.zeros(line, F32)] * 3
    for chip in range(chips):
        parts = [
            jnp.where(left[:1], border_got[1, chip, pl.ds(n, 1)], border_got[0, chip, pl.ds(n, 1)]) for n in range(5)
        ]
        color, reach, coarse = color + fine * parts[0], reach + fine * parts[1], coarse + plain * parts[3]
        fine, plain = fine * parts[2], plain * parts[4]
    there = jnp.where(left, jnp.where(col < columns - 1, 1.0, 0.0), jnp.where(col > 0, 1.0, 0.0))
    for n, row in enumerate((color, (reach - SHIFT * (1.0 - fine)) * (1.0 / 2048), coarse)):
        row = jnp.where(there > 0.5, jnp.broadcast_to(row, (8, LANES)), 0.0)
        image_out[n, pl.ds(2 * 8, 8)] = pltpu.roll(row, LANES // 2, 1)


def smooth_kernel(image, color_out, depth_out, coarse_out, padded):
    half = LANES // 2
    for n, out in enumerate((color_out, depth_out, coarse_out)):
        whole = image[n]
        turned = pltpu.roll(whole, half, 1)
        padded[n, pl.ds(7, 1)] = whole[16:17]
        padded[n, pl.ds(8, HALF)] = whole[:HALF]
        padded[n, pl.ds(8 + HALF, HALF)] = turned[:HALF]
        padded[n, pl.ds(8 + 2 * HALF, 1)] = turned[16:17]
        smooth = 0.25 * padded[n, pl.ds(7, 32)] + 0.5 * padded[n, pl.ds(8, 32)] + 0.25 * padded[n, pl.ds(9, 32)]
        out[...] = smooth[:, :half]


def body(field, fine_plane, fine_frac, counts):
    channels, depth, rows, width = field.shape
    slots = fine_plane.shape[0]
    tiles = width // LANES
    dma = pltpu.SemaphoreType.DMA
    out = jax.ShapeDtypeStruct((rows, LANES // 2), F32)
    vmem = pl.BlockSpec(memory_space=pltpu.VMEM)
    anywhere = pl.BlockSpec(memory_space=pltpu.HBM)
    image = pl.pallas_call(
        kernel,
        out_shape=jax.ShapeDtypeStruct((3, 24, LANES), F32),
        in_specs=[anywhere] * 4,
        out_specs=vmem,
        scratch_shapes=[
            pltpu.VMEM((channels, depth, rows, width), jnp.bfloat16),
            pltpu.VMEM((channels, rows, width), jnp.bfloat16),
            pltpu.VMEM((channels, rows, width), jnp.bfloat16),
            pltpu.VMEM((slots, rows, width), jnp.int32),
            pltpu.VMEM((slots, rows, width), jnp.int32),
            pltpu.VMEM((1, rows, width), jnp.int32),
            pltpu.VMEM((tiles, 3, 5, HALF, LANES), F32),
            pltpu.VMEM((tiles, 5, 8, LANES), jnp.int32),
            pltpu.VMEM((tiles, 5, 8, LANES), jnp.int32),
            pltpu.VMEM((tiles, 8, LANES), F32),
            pltpu.VMEM((2, tiles, 8, LANES), F32),
            dma((4, tiles + 1)),
            dma((tiles,)), dma((tiles,)),
            dma((tiles,)), dma((tiles,)),
            dma((tiles,)), dma((tiles,)),
            dma((2, tiles)), dma((2, tiles)),
            pltpu.SemaphoreType.REGULAR, pltpu.SemaphoreType.REGULAR,
        ],
        compiler_params=pltpu.CompilerParams(collective_id=0, has_side_effects=True, vmem_limit_bytes=56400000),
        name="render",
    )(field, fine_plane, fine_frac, counts)
    return pl.pallas_call(
        smooth_kernel,
        out_shape=(out, out, out),
        in_specs=[vmem],
        out_specs=(vmem, vmem, vmem),
        scratch_shapes=[pltpu.VMEM((3, rows + 16, LANES), F32)],
        compiler_params=pltpu.CompilerParams(vmem_limit_bytes=4 << 20),
        name="smooth",
    )(image)


def solution(mesh):
    in_specs = (
        P(None, "slab", "col", None),
        P("slab", "col", None),
        P("slab", "col", None),
        P("slab", "col", None),
    )
    out_specs = (P("col", "slab"), P("col", "slab"), P("col", "slab"))
    return jax.shard_map(body, mesh=mesh, in_specs=in_specs, out_specs=out_specs, check_vma=False)
```

time: 26.1 us -> 24.3 us (0.931)
  the two profiles are of different devices: /device:TPU:31 before, /device:TPU:1 now
where the time goes in v1:
time: 24.3 us; the launch traced here: 24.1 us
  Pallas kernels  23.5 us (97%)
  between operations  0.64 us (3%)
    pallas_call x1, Pallas kernels, body(): pl.pallas_call(kernel, out_shape=jax.ShapeDtypeStruct((3, 24, LANES), F32...  22.8 us
    pallas_call x1, Pallas kernels, body(): pl.pallas_call(smooth_kernel, out_shape=(out, out, out), in_specs=[vmem],...  0.7 us

profile of v1, /device:TPU:1, one launch (start us, length us, event | category | flops | bytes accessed | tf_op | source)
XLA Modules:
  0.0 24.1 jit_solution(15474798648849797663)
XLA Ops:
  0.6 22.8 %render.1.image = f32[3,24,128]{2,1,0:T(8,128)S(1)} custom-call(bf16[2,16,32,1024]{3,2,1,0:T(8,128)(2,1)} %field_in.1, s32[8,32,1024]{2,1,0:T(8,128)} %plane_in.1, s32[8,32,1024]{2,1,0:T(8,128)} %frac_in.1, s32[1,32,1024]{2,1,0:T(8,128)} %count_in.1), custom_call_target="tpu_custom_call" | custom-call | tf_op jit(solution)/shard_map/render/pallas_call | solution.py:419
  23.4 0.7 %smooth.1 = (f32[32,64]{1,0:T(8,128)}, f32[32,64]{1,0:T(8,128)}, f32[32,64]{1,0:T(8,128)}) custom-call(f32[3,24,128]{2,1,0:T(8,128)S(1)} %render.1.image), custom_call_target="tpu_custom_call" | custom-call | tf_op jit(solution)/shard_map/smooth/pallas_call | solution.py:446

commit v2 on v1

--- a/solution.py
+++ b/solution.py
@@ -8,6 +8,7 @@
 F32 = jnp.float32
 MESH = pl.DeviceIdType.MESH
 LANES = 128
+LEADERS = 3
 HALF = 16
 LOG2E = 1.4426950408889634
 SHIFT = 0.5
@@ -92,7 +93,7 @@
     field_in, plane_in, frac_in, count_in,
     image_out,
     field, front, halo, planes, fracs, counts, pool, packed, got, border, border_got,
-    load_sem, halo_send, halo_recv, pair_send, pair_recv, chip_send, chip_recv, border_send, border_recv, behind, told,
+    load_sem, halo_send, halo_recv, pair_send, pair_recv, chip_send, chip_recv, border_send, border_recv, behind, level, told,
 ):
     slab, col = lax.axis_index("slab"), lax.axis_index("col")
     slabs, columns = lax.axis_size("slab"), lax.axis_size("col")
@@ -107,25 +108,35 @@
     def lanes(tile):
         return pl.ds(pl.multiple_of(tile * LANES, LANES), LANES)
 
-    def loads(i):
-        cols = lanes(i)
+    spans = [(0, 1), (1, tiles // 2), (tiles // 2, tiles)]
+
+    def span(first, last):
+        return pl.ds(first * LANES, (last - first) * LANES)
+
+    def loads(n, cols):
         return [
-            pltpu.make_async_copy(field_in.at[:, :, :, cols], field.at[:, :, :, cols], load_sem.at[0, i]),
-            pltpu.make_async_copy(plane_in.at[:, :, cols], planes.at[:, :, cols], load_sem.at[1, i]),
-            pltpu.make_async_copy(frac_in.at[:, :, cols], fracs.at[:, :, cols], load_sem.at[2, i]),
-            pltpu.make_async_copy(count_in.at[:, :, cols], counts.at[:, :, cols], load_sem.at[3, i]),
+            pltpu.make_async_copy(field_in.at[:, :, :, cols], field.at[:, :, :, cols], load_sem.at[0, n]),
+            pltpu.make_async_copy(plane_in.at[:, :, cols], planes.at[:, :, cols], load_sem.at[1, n]),
+            pltpu.make_async_copy(frac_in.at[:, :, cols], fracs.at[:, :, cols], load_sem.at[2, n]),
+            pltpu.make_async_copy(count_in.at[:, :, cols], counts.at[:, :, cols], load_sem.at[3, n]),
         ]
+
+    first_load, other_load = loads(0, span(0, 1)), loads(1, span(1, tiles))
 
     barrier = pltpu.get_barrier_semaphore()
 
     def tell(semaphore, s, c):
         pl.semaphore_signal(semaphore, inc=1, device_id=device(s, c), device_id_type=MESH)
 
-    first_plane = pltpu.make_async_copy(field_in.at[:, 0], front, load_sem.at[0, tiles])
+    first_plane = [
+        pltpu.make_async_copy(field_in.at[:, 0, :, cols], front.at[:, :, cols], load_sem.at[4, n])
+        for n, cols in enumerate((span(0, 1), span(1, tiles)))
+    ]
 
     @pl.when(slab > 0)
     def _():
-        first_plane.start()
+        for copy in first_plane:
+            copy.start()
 
     tell(barrier, other, col)
 
@@ -133,11 +144,11 @@
     def _():
         tell(barrier, slab + 1, col)
 
-    for copy in loads(0):
+    for copy in first_load:
         copy.start()
 
     def tell_behind(chip, _):
-        tell(barrier, 2 * chip + core, col)
+        tell(barrier, 2 * chip + 1, col)
         return 0
 
     lax.fori_loop(z + 1, chips, tell_behind, 0)
@@ -156,59 +167,50 @@
             tell(barrier, 2 * chip + 1, c)
             return 0
 
-        lax.fori_loop(z, chips, tell_beside, 0)
+        lax.fori_loop(jnp.where(z == 0, 0, jnp.where(z < LEADERS, z + 1, chips)), chips, tell_beside, 0)
 
     both_sides(greet_side)
+
+    for copy in other_load:
+        copy.start()
 
     def count(*conditions):
         return sum(jnp.where(c, 1, 0) for c in conditions)
 
     sides = count(col > 0, col < columns - 1)
-    pl.semaphore_wait(barrier, 1 + z + (1 - core) * count(z > 0) + core * 2 * (z + 1) * sides)
-
-    def front_copy(to, i):
-        cols = lanes(i)
+    pl.semaphore_wait(barrier, 1 + jnp.where(core == 1, 2 * z + 2 * jnp.clip(z, 1, LEADERS) * sides, count(z > 0)))
+
+    def front_copy(to, n):
+        cols = span(*spans[n])
         return pltpu.make_async_remote_copy(
             src_ref=front.at[:, :, cols], dst_ref=halo.at[:, :, cols],
-            send_sem=halo_send.at[i], recv_sem=halo_recv.at[i],
+            send_sem=halo_send, recv_sem=halo_recv.at[n],
             device_id=device(to, col), device_id_type=MESH,
         )
 
     @pl.when(slab > 0)
     def _():
-        first_plane.wait()
-
-        def start_front(i, _):
-            front_copy(slab - 1, i).start()
-            return 0
-
-        lax.fori_loop(0, tiles, start_front, 0)
+        first_plane[0].wait()
+        front_copy(slab - 1, 0).start()
+        first_plane[1].wait()
+        for n in range(1, len(spans)):
+            front_copy(slab - 1, n).start()
 
     def told_ahead(chip, _):
         tell(behind, 2 * chip + core, col)
         return 0
 
     def aside(side, c):
-        def told_aside(chip, _):
-            tell(behind, 2 * chip + core, c)
-            return 0
-
-        lax.fori_loop(0, z, told_aside, 0)
-
-    lax.fori_loop(0, z, told_ahead, 0)
+        @pl.when(z > 0)
+        def _():
+            tell(behind, core, c)
 
     @pl.when(core == 1)
     def _():
         tell(told, other, col)
+        lax.fori_loop(0, z, told_ahead, 0)
         both_sides(aside)
 
-    def start_loads(i, _):
-        for copy in loads(i):
-            copy.start()
-        return 0
-
-    lax.fori_loop(1, tiles, start_loads, 0)
-
     @pl.when(slab == slabs - 1)
     def _():
         halo[...] = jnp.zeros_like(halo)
@@ -216,26 +218,27 @@
     @pl.when(core == 0)
     def _():
         pl.semaphore_wait(told, 1)
+        lax.fori_loop(0, z, told_ahead, 0)
         both_sides(aside)
 
     def pair_copy(i):
         return pltpu.make_async_remote_copy(
             src_ref=pool.at[i, 2], dst_ref=pool.at[i, core],
-            send_sem=pair_send.at[i], recv_sem=pair_recv.at[i],
+            send_sem=pair_send, recv_sem=pair_recv.at[i],
             device_id=device(other, col), device_id_type=MESH,
         )
 
     def chip_copy(i):
         return pltpu.make_async_remote_copy(
             src_ref=packed.at[i], dst_ref=got.at[z],
-            send_sem=chip_send.at[i], recv_sem=chip_recv.at[z],
+            send_sem=chip_send, recv_sem=chip_recv.at[z],
             device_id=device(2 * i + core, col), device_id_type=MESH,
         )
 
     def border_copy(i, side, c):
         return pltpu.make_async_remote_copy(
             src_ref=border.at[i], dst_ref=border_got.at[1 - side, z],
-            send_sem=border_send.at[side, i], recv_sem=border_recv.at[1 - side, z],
+            send_sem=border_send.at[side], recv_sem=border_recv.at[1 - side],
             device_id=device(2 * i + core, c), device_id_type=MESH,
         )
 
@@ -243,14 +246,12 @@
     left_slot = jnp.where(core == 0, 0, 2)
     right_slot = jnp.where(core == 0, 2, 1)
 
+    def hear_front(n):
+        @pl.when(slab < slabs - 1)
+        def _():
+            front_copy(slab, n).wait_recv()
+
     def march(i):
-        for copy in loads(i):
-            copy.wait()
-
-        @pl.when(slab < slabs - 1)
-        def _():
-            front_copy(slab, i).wait_recv()
-
         parts = [
             march_group(field, halo, planes, fracs, counts, pl.ds(HALF * g, HALF), lanes(i), slab) for g in range(2)
         ]
@@ -290,58 +291,68 @@
             for n, word in enumerate(words):
                 packed[i, n] = word
 
-    def send(i):
-        @pl.when(i != z)
-        def _():
-            chip_copy(i).start()
-
+    def send_border(i):
         both_sides(lambda side, c: border_copy(i, side, c).start())
 
     def finish(i):
         join(i)
 
-        @pl.when(i <= z)
-        def _():
-            send(i)
+        @pl.when(i < z)
+        def _():
+            chip_copy(i).start()
+
+        @pl.when(i < jnp.minimum(z, LEADERS))
+        def _():
+            send_border(i)
 
     def step(i, _):
+        @pl.when(i == tiles // 2)
+        def _():
+            hear_front(2)
+
         march(i)
         finish(i - 1)
         return 0
 
+    for copy in first_load:
+        copy.wait()
+    hear_front(0)
     march(0)
-    lax.fori_loop(1, tiles, step, 0)
+    finish(0)
+    for copy in other_load:
+        copy.wait()
+    hear_front(1)
+    march(1)
+    lax.fori_loop(2, tiles, step, 0)
     finish(tiles - 1)
 
     @pl.when(z < chips - 1)
     def _():
-        pl.semaphore_wait(behind, (chips - 1 - z) * (1 + sides))
-
-        def send_behind(i, _):
-            send(i)
+        pl.semaphore_wait(behind, (chips - 1 - z) * jnp.where(z == 0, 1 + sides, 1))
+
+    @pl.when(z == 0)
+    def _():
+        def tell_level(chip, _):
+            tell(level, 2 * chip + core, col)
             return 0
 
-        lax.fori_loop(z + 1, chips, send_behind, 0)
-
-    @pl.when(slab > 0)
-    def _():
-        def end_front(i, _):
-            front_copy(slab - 1, i).wait_send()
-            return 0
-
-        lax.fori_loop(0, tiles, end_front, 0)
-
-    def end_tile(i, _):
-        pair_copy(i).wait_send()
-
-        @pl.when(i != z)
-        def _():
-            chip_copy(i).wait_send()
-
-        both_sides(lambda side, c: border_copy(i, side, c).wait_send())
+        lax.fori_loop(1, chips, tell_level, 0)
+
+    def send_behind(i, _):
+        chip_copy(i).start()
         return 0
 
-    lax.fori_loop(0, tiles, end_tile, 0)
+    lax.fori_loop(z + 1, chips, send_behind, 0)
+
+    @pl.when(z > 0)
+    def _():
+        pl.semaphore_wait(level, 1)
+
+    def send_beside(i, _):
+        send_border(i)
+        return 0
+
+    lax.fori_loop(jnp.minimum(z, LEADERS), chips, send_beside, 0)
 
     shape = (8, LANES)
     state = [[jnp.ones(shape, F32), jnp.ones(shape, F32)] + [jnp.zeros(shape, F32)] * 3 for _ in range(2)]
@@ -350,7 +361,7 @@
         @pl.when(z != chip)
         def _():
             pltpu.make_async_remote_copy(
-                src_ref=packed.at[0], dst_ref=got.at[chip], send_sem=chip_send.at[0], recv_sem=chip_recv.at[chip],
+                src_ref=packed.at[0], dst_ref=got.at[chip], send_sem=chip_send, recv_sem=chip_recv.at[chip],
                 device_id=device(slab, col), device_id_type=MESH,
             ).wait_recv()
 
@@ -371,15 +382,13 @@
         image_out[1, rows] = (reach - SHIFT * (1.0 - fine)) * (1.0 / 2048)
         image_out[2, rows] = coarse
 
-    def border_waits(side, c):
-        for chip in range(chips):
-            pltpu.make_async_remote_copy(
-                src_ref=border.at[0], dst_ref=border_got.at[side, chip],
-                send_sem=border_send.at[side, 0], recv_sem=border_recv.at[side, chip],
-                device_id=device(slab, c), device_id_type=MESH,
-            ).wait_recv()
-
-    both_sides(border_waits)
+    def all_borders(side, c):
+        return pltpu.make_async_remote_copy(
+            src_ref=border, dst_ref=border_got.at[side], send_sem=border_send.at[side], recv_sem=border_recv.at[side],
+            device_id=device(slab, c), device_id_type=MESH,
+        )
+
+    both_sides(lambda side, c: all_borders(side, c).wait_recv())
     line = (1, LANES)
     fine, plain = jnp.ones(line, F32), jnp.ones(line, F32)
     color, reach, coarse = [jnp.zeros(line, F32)] * 3
@@ -393,6 +402,24 @@
     for n, row in enumerate((color, (reach - SHIFT * (1.0 - fine)) * (1.0 / 2048), coarse)):
         row = jnp.where(there > 0.5, jnp.broadcast_to(row, (8, LANES)), 0.0)
         image_out[n, pl.ds(2 * 8, 8)] = pltpu.roll(row, LANES // 2, 1)
+
+    @pl.when(slab > 0)
+    def _():
+        pltpu.make_async_remote_copy(
+            src_ref=front, dst_ref=halo, send_sem=halo_send, recv_sem=halo_recv.at[0],
+            device_id=device(slab - 1, col), device_id_type=MESH,
+        ).wait_send()
+
+    pltpu.make_async_remote_copy(
+        src_ref=pool.at[:, 2], dst_ref=pool.at[:, core], send_sem=pair_send, recv_sem=pair_recv.at[0],
+        device_id=device(other, col), device_id_type=MESH,
+    ).wait_send()
+    others = pl.ds(0, tiles - 1)
+    pltpu.make_async_remote_copy(
+        src_ref=packed.at[others], dst_ref=got.at[others], send_sem=chip_send, recv_sem=chip_recv.at[0],
+        device_id=device(other, col), device_id_type=MESH,
+    ).wait_send()
+    both_sides(lambda side, c: all_borders(side, c).wait_send())
 
 
 def smooth_kernel(image, color_out, depth_out, coarse_out, padded):
@@ -433,12 +460,12 @@
             pltpu.VMEM((tiles, 5, 8, LANES), jnp.int32),
             pltpu.VMEM((tiles, 8, LANES), F32),
             pltpu.VMEM((2, tiles, 8, LANES), F32),
-            dma((4, tiles + 1)),
-            dma((tiles,)), dma((tiles,)),
-            dma((tiles,)), dma((tiles,)),
-            dma((tiles,)), dma((tiles,)),
-            dma((2, tiles)), dma((2, tiles)),
-            pltpu.SemaphoreType.REGULAR, pltpu.SemaphoreType.REGULAR,
+            dma((5, 2)),
+            dma, dma((3,)),
+            dma, dma((tiles,)),
+            dma, dma((tiles,)),
+            dma((2,)), dma((2,)),
+            pltpu.SemaphoreType.REGULAR, pltpu.SemaphoreType.REGULAR, pltpu.SemaphoreType.REGULAR,
         ],
         compiler_params=pltpu.CompilerParams(collective_id=0, has_side_effects=True, vmem_limit_bytes=56400000),
         name="render",

time: 24.3 us -> 23.2 us (0.955)
  the two profiles are of different devices: /device:TPU:1 before, /device:TPU:240 now
where the time goes in v2:
time: 23.2 us; the launch traced here: 23.1 us
  Pallas kernels  22.5 us (97%)
  between operations  0.64 us (3%)
    pallas_call x1, Pallas kernels, body(): pl.pallas_call(kernel, out_shape=jax.ShapeDtypeStruct((3, 24, LANES), F32...  21.8 us
    pallas_call x1, Pallas kernels, body(): pl.pallas_call(smooth_kernel, out_shape=(out, out, out), in_specs=[vmem],...  0.7 us

profile of v2, /device:TPU:240, one launch (start us, length us, event | category | flops | bytes accessed | tf_op | source)
XLA Modules:
  0.0 23.1 jit_solution(14549660403482574127)
XLA Ops:
  0.6 21.8 %render.1.image = f32[3,24,128]{2,1,0:T(8,128)S(1)} custom-call(bf16[2,16,32,1024]{3,2,1,0:T(8,128)(2,1)} %field_in.1, s32[8,32,1024]{2,1,0:T(8,128)} %plane_in.1, s32[8,32,1024]{2,1,0:T(8,128)} %frac_in.1, s32[1,32,1024]{2,1,0:T(8,128)} %count_in.1), custom_call_target="tpu_custom_call" | custom-call | tf_op jit(solution)/shard_map/render/pallas_call | solution.py:446
  22.4 0.7 %smooth.1 = (f32[32,64]{1,0:T(8,128)}, f32[32,64]{1,0:T(8,128)}, f32[32,64]{1,0:T(8,128)}) custom-call(f32[3,24,128]{2,1,0:T(8,128)S(1)} %render.1.image), custom_call_target="tpu_custom_call" | custom-call | tf_op jit(solution)/shard_map/smooth/pallas_call | solution.py:473

commit v3 on v2

--- a/solution.py
+++ b/solution.py
@@ -8,7 +8,8 @@
 F32 = jnp.float32
 MESH = pl.DeviceIdType.MESH
 LANES = 128
-LEADERS = 3
+AHEAD = 5
+LEADERS = 4
 HALF = 16
 LOG2E = 1.4426950408889634
 SHIFT = 0.5
@@ -167,7 +168,7 @@
             tell(barrier, 2 * chip + 1, c)
             return 0
 
-        lax.fori_loop(jnp.where(z == 0, 0, jnp.where(z < LEADERS, z + 1, chips)), chips, tell_beside, 0)
+        lax.fori_loop(jnp.where(z < LEADERS, z + 1, chips), chips, tell_beside, 0)
 
     both_sides(greet_side)
 
@@ -178,7 +179,7 @@
         return sum(jnp.where(c, 1, 0) for c in conditions)
 
     sides = count(col > 0, col < columns - 1)
-    pl.semaphore_wait(barrier, 1 + jnp.where(core == 1, 2 * z + 2 * jnp.clip(z, 1, LEADERS) * sides, count(z > 0)))
+    pl.semaphore_wait(barrier, 1 + jnp.where(core == 1, 2 * z + 2 * jnp.minimum(z, LEADERS) * sides, count(z > 0)))
 
     def front_copy(to, n):
         cols = span(*spans[n])
@@ -208,6 +209,12 @@
     @pl.when(core == 1)
     def _():
         tell(told, other, col)
+
+        @pl.when(z == 1)
+        def _():
+            tell(level, 0, col)
+            tell(level, 1, col)
+
         lax.fori_loop(0, z, told_ahead, 0)
         both_sides(aside)
 
@@ -305,26 +312,33 @@
         def _():
             send_border(i)
 
+    lag = jnp.where(z == chips - 1, 1, jnp.where(core == 0, AHEAD, 0))
+
     def step(i, _):
+        @pl.when(i == 1)
+        def _():
+            for copy in other_load:
+                copy.wait()
+            hear_front(1)
+
         @pl.when(i == tiles // 2)
         def _():
             hear_front(2)
 
-        march(i)
-        finish(i - 1)
+        @pl.when(i < tiles)
+        def _():
+            march(i)
+
+        @pl.when(i >= lag)
+        def _():
+            finish(i - lag)
+
         return 0
 
     for copy in first_load:
         copy.wait()
     hear_front(0)
-    march(0)
-    finish(0)
-    for copy in other_load:
-        copy.wait()
-    hear_front(1)
-    march(1)
-    lax.fori_loop(2, tiles, step, 0)
-    finish(tiles - 1)
+    lax.fori_loop(0, tiles + lag, step, 0)
 
     @pl.when(z < chips - 1)
     def _():
@@ -344,9 +358,7 @@
 
     lax.fori_loop(z + 1, chips, send_behind, 0)
 
-    @pl.when(z > 0)
-    def _():
-        pl.semaphore_wait(level, 1)
+    pl.semaphore_wait(level, 1)
 
     def send_beside(i, _):
         send_border(i)

time: 23.2 us -> 21.7 us (0.935)
  the two profiles are of different devices: /device:TPU:240 before, /device:TPU:51 now
where the time goes in v3:
time: 21.7 us; the launch traced here: 21.6 us
  Pallas kernels  20.9 us (96%)
  between operations  0.64 us (3%)
    pallas_call x1, Pallas kernels, body(): pl.pallas_call(kernel, out_shape=jax.ShapeDtypeStruct((3, 24, LANES), F32...  20.2 us
    pallas_call x1, Pallas kernels, body(): pl.pallas_call(smooth_kernel, out_shape=(out, out, out), in_specs=[vmem],...  0.7 us

profile of v3, /device:TPU:51, one launch (start us, length us, event | category | flops | bytes accessed | tf_op | source)
XLA Modules:
  0.0 21.6 jit_solution(2660885085764153094)
XLA Ops:
  0.6 20.2 %render.1.image = f32[3,24,128]{2,1,0:T(8,128)S(1)} custom-call(bf16[2,16,32,1024]{3,2,1,0:T(8,128)(2,1)} %field_in.1, s32[8,32,1024]{2,1,0:T(8,128)} %plane_in.1, s32[8,32,1024]{2,1,0:T(8,128)} %frac_in.1, s32[1,32,1024]{2,1,0:T(8,128)} %count_in.1), custom_call_target="tpu_custom_call" | custom-call | tf_op jit(solution)/shard_map/render/pallas_call | solution.py:458
  20.9 0.7 %smooth.1 = (f32[32,64]{1,0:T(8,128)}, f32[32,64]{1,0:T(8,128)}, f32[32,64]{1,0:T(8,128)}) custom-call(f32[3,24,128]{2,1,0:T(8,128)S(1)} %render.1.image), custom_call_target="tpu_custom_call" | custom-call | tf_op jit(solution)/shard_map/smooth/pallas_call | solution.py:485

commit v4 on v3

--- a/solution.py
+++ b/solution.py
@@ -8,8 +8,8 @@
 F32 = jnp.float32
 MESH = pl.DeviceIdType.MESH
 LANES = 128
-AHEAD = 5
-LEADERS = 4
+AHEAD = 4
+LEADERS = 3
 HALF = 16
 LOG2E = 1.4426950408889634
 SHIFT = 0.5
@@ -308,9 +308,15 @@
         def _():
             chip_copy(i).start()
 
-        @pl.when(i < jnp.minimum(z, LEADERS))
-        def _():
-            send_border(i)
+        @pl.when(jnp.logical_and(z > LEADERS, i == LEADERS))
+        def _():
+            pl.semaphore_wait(level, 1)
+
+        @pl.when(jnp.logical_or(z > LEADERS, i < z))
+        def _():
+            @pl.when(jnp.logical_or(z > LEADERS, i < LEADERS))
+            def _():
+                send_border(i)
 
     lag = jnp.where(z == chips - 1, 1, jnp.where(core == 0, AHEAD, 0))
 
@@ -358,13 +364,15 @@
 
     lax.fori_loop(z + 1, chips, send_behind, 0)
 
-    pl.semaphore_wait(level, 1)
-
-    def send_beside(i, _):
-        send_border(i)
-        return 0
-
-    lax.fori_loop(jnp.minimum(z, LEADERS), chips, send_beside, 0)
+    @pl.when(z <= LEADERS)
+    def _():
+        pl.semaphore_wait(level, 1)
+
+        def send_beside(i, _):
+            send_border(i)
+            return 0
+
+        lax.fori_loop(z, chips, send_beside, 0)
 
     shape = (8, LANES)
     state = [[jnp.ones(shape, F32), jnp.ones(shape, F32)] + [jnp.zeros(shape, F32)] * 3 for _ in range(2)]

time: 21.7 us -> 21.3 us (0.982)
  the two profiles are of different devices: /device:TPU:51 before, /device:TPU:56 now
where the time goes in v4:
time: 21.3 us; the launch traced here: 21.2 us
  Pallas kernels  20.6 us (97%)
  between operations  0.64 us (3%)
    pallas_call x1, Pallas kernels, body(): pl.pallas_call(kernel, out_shape=jax.ShapeDtypeStruct((3, 24, LANES), F32...  19.9 us
    pallas_call x1, Pallas kernels, body(): pl.pallas_call(smooth_kernel, out_shape=(out, out, out), in_specs=[vmem],...  0.7 us

profile of v4, /device:TPU:56, one launch (start us, length us, event | category | flops | bytes accessed | tf_op | source)
XLA Modules:
  0.0 21.2 jit_solution(4290987549448249815)
XLA Ops:
  0.6 19.9 %render.1.image = f32[3,24,128]{2,1,0:T(8,128)S(1)} custom-call(bf16[2,16,32,1024]{3,2,1,0:T(8,128)(2,1)} %field_in.1, s32[8,32,1024]{2,1,0:T(8,128)} %plane_in.1, s32[8,32,1024]{2,1,0:T(8,128)} %frac_in.1, s32[1,32,1024]{2,1,0:T(8,128)} %count_in.1), custom_call_target="tpu_custom_call" | custom-call | tf_op jit(solution)/shard_map/render/pallas_call | solution.py:466
  20.5 0.7 %smooth.1 = (f32[32,64]{1,0:T(8,128)}, f32[32,64]{1,0:T(8,128)}, f32[32,64]{1,0:T(8,128)}) custom-call(f32[3,24,128]{2,1,0:T(8,128)S(1)} %render.1.image), custom_call_target="tpu_custom_call" | custom-call | tf_op jit(solution)/shard_map/smooth/pallas_call | solution.py:493

commit v5 on v4

--- a/solution.py
+++ b/solution.py
@@ -304,10 +304,6 @@
     def finish(i):
         join(i)
 
-        @pl.when(i < z)
-        def _():
-            chip_copy(i).start()
-
         @pl.when(jnp.logical_and(z > LEADERS, i == LEADERS))
         def _():
             pl.semaphore_wait(level, 1)
@@ -317,6 +313,10 @@
             @pl.when(jnp.logical_or(z > LEADERS, i < LEADERS))
             def _():
                 send_border(i)
+
+        @pl.when(i < z)
+        def _():
+            chip_copy(i).start()
 
     lag = jnp.where(z == chips - 1, 1, jnp.where(core == 0, AHEAD, 0))
 

time: 21.3 us -> 21.3 us (level)
  no operation moved by 1% of the time
where the time goes in v5:
time: 21.3 us; the launch traced here: 21.2 us
  Pallas kernels  20.6 us (97%)
  between operations  0.64 us (3%)
    pallas_call x1, Pallas kernels, body(): pl.pallas_call(kernel, out_shape=jax.ShapeDtypeStruct((3, 24, LANES), F32...  19.9 us
    pallas_call x1, Pallas kernels, body(): pl.pallas_call(smooth_kernel, out_shape=(out, out, out), in_specs=[vmem],...  0.7 us

profile of v5, /device:TPU:56, one launch (start us, length us, event | category | flops | bytes accessed | tf_op | source)
XLA Modules:
  0.0 21.2 jit_solution(2667879543325598633)
XLA Ops:
  0.6 19.9 %render.1.image = f32[3,24,128]{2,1,0:T(8,128)S(1)} custom-call(bf16[2,16,32,1024]{3,2,1,0:T(8,128)(2,1)} %field_in.1, s32[8,32,1024]{2,1,0:T(8,128)} %plane_in.1, s32[8,32,1024]{2,1,0:T(8,128)} %frac_in.1, s32[1,32,1024]{2,1,0:T(8,128)} %count_in.1), custom_call_target="tpu_custom_call" | custom-call | tf_op jit(solution)/shard_map/render/pallas_call | solution.py:466
  20.5 0.7 %smooth.1 = (f32[32,64]{1,0:T(8,128)}, f32[32,64]{1,0:T(8,128)}, f32[32,64]{1,0:T(8,128)}) custom-call(f32[3,24,128]{2,1,0:T(8,128)S(1)} %render.1.image), custom_call_target="tpu_custom_call" | custom-call | tf_op jit(solution)/shard_map/smooth/pallas_call | solution.py:493
